TPU v7x, 512 devices: a whole 4x8x8 slice. The times are simulated.
512 devices in a mesh: outer: 16 (over y, core), inner: 32 (over x, z).
Axes of the slice: x: 4, y: 8, z: 8, core: 2. Of those that a mesh axis runs over, the one named last changes fastest.
Arguments:
- queries: bfloat16 [32768, 4096], P('inner', 'outer'), may hold values from -150 to 150
- keys: bfloat16 [32768, 4096], P('inner', 'outer'), may hold values from -7 to 7
- values: bfloat16 [32768, 4096], P('inner', 'outer'), may hold values from -18 to 18
- counts: int32 [256], P('inner'), may hold values from 1 to 128, 24576 in all
- window_mask: int32 [256, 3], P('inner'), may hold values 0 or 1
- norm_gain: float32 [4096], P('outer'), may hold values from 0.5 to 1.5
Outputs:
- attended: bfloat16 [32768, 4096], P('inner', 'outer')
Inputs may be any that keep to these rules, and one draw needn't show every extreme that they name: `counts`: the largest count is exactly 128.
All inputs are finite; a program needn't handle non-finite values. No bound on the sum of `counts` or of `window_mask` on one device may be relied on, other than what follows from the above.
Results may differ from a plain program's by a relative error of at most 0.0048.
Values may be sent and summed in bfloat16 or wider, within the bound.
A program may use at most 64 MiB of HBM per device.

v0:
```python
import jax
import jax.numpy as jnp
from jax import lax
from jax.sharding import PartitionSpec as P

HD = 128
BLK = 128
PREV = 3
WIDTH = 4096


def carried_in(part, axis, combine, identity):
    place = lax.axis_index(axis)
    gathered = lax.all_gather(part, axis)
    state = jnp.zeros_like(part) + jnp.asarray(identity, part.dtype)

    def one(step, state):
        return combine(state, lax.dynamic_index_in_dim(gathered, step, 0, False))

    return lax.fori_loop(0, place, one, state)


def from_behind(value, axis, steps):
    count = lax.axis_size(axis)
    first, last = (max(0, -steps), min(count, count - steps))
    return lax.ppermute(value, axis, [(source, source + steps) for source in range(first, last)])


def add_states(earlier, later):
    return earlier + later


def shards(queries, keys, values, counts, window_mask, norm_gain):
    tok_rows = queries.shape[0]
    groups_here = tok_rows // BLK
    local_heads = queries.shape[1] // HD
    position = lax.broadcasted_iota(jnp.int32, (BLK,), 0)
    key_valid = position[None, :] < counts[:, None]
    masked_keys = jnp.where(key_valid.reshape(tok_rows)[:, None], keys, jnp.zeros((), jnp.bfloat16))
    query_blocks = queries.reshape(groups_here, BLK, local_heads, HD)
    key_blocks = masked_keys.reshape(groups_here, BLK, local_heads, HD)
    value_blocks = values.reshape(groups_here, BLK, local_heads, HD)
    group_states = jnp.einsum(
        "cshd,cshe->chde", key_blocks, value_blocks, preferred_element_type=jnp.float32
    )
    running = jnp.cumsum(group_states, axis=0)
    within = jnp.concatenate([jnp.zeros_like(group_states[:1]), running[:-1]], axis=0)
    span_total = running[-1]
    before = carried_in(span_total, "inner", add_states, jnp.zeros_like(span_total))
    prior_rounded = (before[None] + within).astype(jnp.bfloat16)
    rim_rows = PREV * BLK
    rim_keys, rim_values, rim_counts = from_behind(
        (
            masked_keys[tok_rows - rim_rows :],
            values[tok_rows - rim_rows :],
            counts[groups_here - PREV :],
        ),
        "inner",
        1,
    )
    extended_keys = jnp.concatenate([rim_keys, masked_keys], axis=0).reshape(
        groups_here + PREV, BLK, local_heads, HD
    )
    extended_values = jnp.concatenate([rim_values, values], axis=0).reshape(
        groups_here + PREV, BLK, local_heads, HD
    )
    extended_counts = jnp.concatenate([rim_counts, counts], axis=0)
    extended_valid = position[None, :] < extended_counts[:, None]
    window_keys = jnp.stack(
        [extended_keys[place : place + groups_here] for place in range(PREV + 1)], axis=1
    ).reshape(groups_here, (PREV + 1) * BLK, local_heads, HD)
    window_values = jnp.stack(
        [extended_values[place : place + groups_here] for place in range(PREV + 1)], axis=1
    ).reshape(groups_here, (PREV + 1) * BLK, local_heads, HD)
    window_valid = jnp.stack(
        [extended_valid[place : place + groups_here] for place in range(PREV + 1)], axis=1
    )
    group_on = jnp.concatenate(
        [window_mask[:, ::-1] == 1, jnp.ones((groups_here, 1), jnp.bool_)], axis=1
    )
    causal = position[:, None] >= position[None, :]
    causal_full = jnp.concatenate([jnp.ones((BLK, PREV * BLK), jnp.bool_), causal], axis=1)
    allowed = (window_valid & group_on[:, :, None]).reshape(
        groups_here, 1, (PREV + 1) * BLK
    ) & causal_full[None]
    score_scale = 1.0 / HD**0.5
    scores = (
        jnp.einsum("cthd,cshd->chts", query_blocks, window_keys, preferred_element_type=jnp.float32)
        * score_scale
    )
    scores = jnp.where(allowed[:, None], scores, -1e30)
    largest = jnp.max(scores, axis=-1, keepdims=True)
    expd = jnp.exp(scores - largest)
    weights = (expd / jnp.sum(expd, axis=-1, keepdims=True)).astype(jnp.bfloat16)
    local_part = jnp.einsum(
        "chts,cshd->cthd", weights, window_values, preferred_element_type=jnp.float32
    )
    inter = jnp.einsum(
        "cthd,chde->cthe", query_blocks, prior_rounded, preferred_element_type=jnp.float32
    )
    intra_weights = jnp.einsum(
        "cthd,cshd->chts", query_blocks, key_blocks, preferred_element_type=jnp.float32
    )
    intra_weights = jnp.where(causal[None, None], intra_weights, 0.0).astype(jnp.bfloat16)
    intra = jnp.einsum(
        "chts,cshe->cthe", intra_weights, value_blocks, preferred_element_type=jnp.float32
    )
    linear_part = inter + intra
    local_squares = jnp.sum(linear_part * linear_part, axis=(2, 3))
    row_squares = lax.psum(local_squares, "outer")
    normed = linear_part * lax.rsqrt(row_squares / WIDTH + 1e-06)[:, :, None, None]
    result = normed * norm_gain.reshape(local_heads, HD)[None, None] + local_part
    return result.reshape(tok_rows, local_heads * HD).astype(jnp.bfloat16)


def solution(mesh):
    return jax.shard_map(
        shards,
        mesh=mesh,
        in_specs=(
            P("inner", "outer"),
            P("inner", "outer"),
            P("inner", "outer"),
            P("inner"),
            P("inner", None),
            P("outer"),
        ),
        out_specs=P("inner", "outer"),
        check_vma=False,
    )
```

profile of v0, /device:TPU:7, one launch (start us, length us, event | category | flops | bytes accessed | tf_op | source)
XLA Modules:
  0.0 166.0 jit_solution(16054141134522092386)
XLA Ops:
  7.3 1.2 broadcast_select_fusion
  8.7 1.2 reshape.85
  13.4 4.0 %collective-permute-start.2 = (bf16[384,256]{1,0:T(8,128)(2,1)}, bf16[384,256]{1,0:T(8,128)(2,1)S(1)}, u32[]{:S(2)}, u32[]{:S(2)}) collective-permute-start(bf16[384,256]{1,0:T(8,128)(2,1)} %slice.79), channel_id=1, source_target_pairs={{0,1},{1,2},{2,3},{3,4},{4,5},{5,6},{6,7},{7,8},{8,9},{9,10},{10,1... | collective-permute-start | bytes 589832 | tf_op jit(solution)/shard_map/ppermute | solution.py:26
  18.1 4.0 %collective-permute-start.1 = (s32[3]{0:T(128)}, s32[3]{0:T(128)}, u32[]{:S(2)}, u32[]{:S(2)}) collective-permute-start(s32[3]{0:T(128)} %slice.61), channel_id=1, source_target_pairs={{0,1},{1,2},{2,3},{3,4},{4,5},{5,6},{6,7},{7,8},{8,9},{9,10},{10,1... | collective-permute-start | bytes 44 | tf_op jit(solution)/shard_map/ppermute | solution.py:26
  22.8 4.0 %collective-permute-start = (bf16[384,256]{1,0:T(8,128)(2,1)}, bf16[384,256]{1,0:T(8,128)(2,1)S(1)}, u32[]{:S(2)}, u32[]{:S(2)}) collective-permute-start(bf16[384,256]{1,0:T(8,128)(2,1)} %slice.57), channel_id=1, source_target_pairs={{0,1},{1,2},{2,3},{3,4},{4,5},{5,6},{6,7},{7,8},{8,9},{9,10},{10,1... | collective-permute-start | bytes 589832 | tf_op jit(solution)/shard_map/ppermute | solution.py:26
  28.6 2.0 %copy.56 = bf16[8,1,128,2,128]{4,2,1,3,0:T(8,128)(2,1)} copy(bf16[8,1,128,2,128]{4,3,2,0,1:T(2,128)(2,1)} %stack.58) | data formatting | bytes 1048576 | tf_op jit(solution)/shard_map/stack | solution.py:69
  30.6 1.2 reshape.86
  31.9 3.8 %copy.52 = bf16[8,1,128,2,128]{2,1,4,3,0:T(2,128)(2,1)} copy(bf16[8,1,128,2,128]{4,3,2,0,1:T(2,128)(2,1)} %stack.48) | data formatting | bytes 1048576 | tf_op jit(solution)/shard_map/stack | solution.py:72
  36.6 1.4 broadcast_and_fusion
  38.9 1.2 stack.55
  44.2 1.2 stack.45
  45.4 2.0 %copy.49 = bf16[8,1,128,2,128]{2,1,4,3,0:T(2,128)(2,1)} copy(bf16[8,1,128,2,128]{4,3,2,0,1:T(2,128)(2,1)S(1)} %stack.45) | data formatting | bytes 1048576 | tf_op jit(solution)/shard_map/stack | solution.py:72
  48.6 2.0 %copy.50 = bf16[8,1,128,2,128]{2,1,4,3,0:T(2,128)(2,1)} copy(bf16[8,1,128,2,128]{4,3,2,0,1:T(2,128)(2,1)S(1)} %stack.46) | data formatting | bytes 1048576 | tf_op jit(solution)/shard_map/stack | solution.py:72
  50.7 2.0 %copy.51 = bf16[8,1,128,2,128]{2,1,4,3,0:T(2,128)(2,1)} copy(bf16[8,1,128,2,128]{4,3,2,0,1:T(2,128)(2,1)S(1)} %stack.47) | data formatting | bytes 1048576 | tf_op jit(solution)/shard_map/stack | solution.py:72
  52.7 6.4 %pad_maximum_fusion = bf16[8,4,128,2,128]{2,1,4,3,0:T(4,128)(2,1)S(1)} fusion(bf16[8,1,128,2,128]{2,1,4,3,0:T(2,128)(2,1)} %copy.52, bf16[8,1,128,2,128]{2,1,4,3,0:T(2,128)(2,1)} %copy.51, bf16[8,1,128,2,128]{2,1,4,3,0:T(2,128)(2,1)} %copy.50, bf16[8,1,128,2,128]{2,1,4,3,0:T(2,128)(2,1)} %copy.49), kind=kLoop, calls=%fused_computation.6 | loop fusion | flops 8388608 | bytes 4194304 | tf_op jit(solution)/shard_map/stack | solution.py:72
  59.1 2.2 %reshape.87 = bf16[8,512,2,128]{1,3,2,0:T(8,128)(2,1)} reshape(bf16[8,4,128,2,128]{2,1,4,3,0:T(4,128)(2,1)S(1)} %pad_maximum_fusion) | data formatting | bytes 4194304 | tf_op jit(solution)/shard_map/reshape | solution.py:74
  61.3 1.8 %pad_maximum_fusion.1 = bf16[8,4,128,2,128]{4,2,1,3,0:T(8,128)(2,1)S(1)} fusion(bf16[8,1,128,2,128]{4,2,1,3,0:T(8,128)(2,1)} %copy.56, bf16[8,1,128,2,128]{4,2,1,3,0:T(8,128)(2,1)} %copy.55, bf16[8,1,128,2,128]{4,2,1,3,0:T(8,128)(2,1)} %copy.54, bf16[8,1,128,2,128]{4,2,1,3,0:T(8,128)(2,1)} %copy.53), kind=kLoop, calls=%fused_computation.7 | loop fusion | flops 3145728 | bytes 4194304 | tf_op jit(solution)/shard_map/stack | solution.py:69
  64.2 3.9 %fusion.33 = (f32[8,2,128]{2,1,0:T(2,128)S(1)}, f32[8,2,128,512]{2,3,1,0:T(8,128)}) fusion(f32[8,2,512,128]{3,2,1,0:T(8,128)S(1)} %fusion.21, pred[8,128,512]{1,2,0:T(8,128)(4,1)S(1)} %copy-done.4), kind=kOutput, calls=%fused_computation.63 | output fusion | flops 6291967 | bytes 8921088 | tf_op jit(solution)/shard_map/sub | solution.py:93
  68.0 32.9 %all-gather.2.cloned.1.call-done = f32[32,2,128,128]{3,2,1,0:T(8,128)} async-done(((f32[1,2,128,128]{3,2,1,0:T(8,128)}), f32[32,2,128,128]{3,2,1,0:T(8,128)}) %all-gather.2.cloned.1.call-update) | async-done | bytes 4194320 | tf_op jit(solution)/shard_map/all_gather | solution.py:14
  100.9 23.1 %while.10 = (s32[]{:T(128)}, f32[2,128,128]{2,1,0:T(8,128)S(1)}, s32[]{:T(128)}, f32[32,2,128,128]{3,2,1,0:T(8,128)}, s32[]{:T(128)}, /*index=5*/s32[]{:T(128)}, s32[]{:T(128)}) while((s32[]{:T(128)}, f32[2,128,128]{2,1,0:T(8,128)S(1)}, s32[]{:T(128)}, f32[32,2,128,128]{3,2,1,0:T(8,128)}, s32[]{:T(128)}, /*index=5*/s32[]{:T(128)}, ...), condition=%wide.region_2.3_spmd, body=%wide.region_1.2_spmd.sunk | while | flops 32773 | bytes 393331 | solution.py:20
  124.1 1.5 convolution_bitcast_fusion.2
  125.6 1.9 %multiply_reduce_fusion = (f32[8,128]{1,0:T(8,128)S(1)}, f32[8,128,2,128]{1,3,2,0:T(8,128)S(1)}) fusion(f32[8,128,2,128]{1,3,2,0:T(8,128)} %convolution_bitcast_fusion.2, bf16[8,128,2,128]{1,3,2,0:T(8,128)(2,1)S(1)} %copy-done.2, pred[128,128]{0,1:T(8,128)(4,1)S(1)} %iota_compare_fusion, bf16[8,128,2,128]{3,2,1,0:T(2,128)(2,1)S(1)} %reshape.84, ...), kind=kOutput, calls=%fused_computation.21 | convolution fusion | flops 135527424 | bytes 3690496 | tf_op jit(solution)/shard_map/chts,cshe->cthe/dot_general | solution.py:105
  127.5 26.7 %psum.7 = f32[8,128]{1,0:T(8,128)S(1)} all-reduce(f32[8,128]{1,0:T(8,128)S(1)} %get-tuple-element.49), channel_id=1, replica_groups=mesh['outer'=16,'inner'=32] {'outer'}, use_global_device_ids=true, to_apply=%region_4.5 | all-reduce | flops 1024 | bytes 8192 | tf_op jit(solution)/shard_map/psum | solution.py:110
  154.2 3.5 %fusion.10 = bf16[8,128,2,128]{1,3,2,0:T(8,128)(2,1)S(1)} fusion(bf16[8,512,2,128]{1,3,2,0:T(8,128)(2,1)} %reshape.87, f32[8,2,128,512]{2,3,1,0:T(8,128)} %get-tuple-element.48, f32[8,2,128]{2,1,0:T(2,128)S(1)} %get-tuple-element.47, f32[8,128,2,128]{1,3,2,0:T(8,128)S(1)} %get-tuple-element.50, f32[2,128]{1,0:T(2,128)S(1)} %bitcast.65, ...), kind=kOutput, calls=%fused_computation.19 | convolution fusion | flops 271581184 | bytes 7877632 | tf_op jit(solution)/shard_map/chts,cshd->cthd/dot_general | solution.py:95
  (83 shorter events, 39.7 us)
Async XLA Ops:
  6.5 94.4 %all-gather.2.cloned.1.call-start = ((), (), s32[]{:S(2)}) async-start(), calls=%async_computation | async-start | bytes 4325376 | tf_op jit(solution)/shard_map/all_gather | solution.py:14
  8.5 8.9 %copy-start.7 = (s32[8]{0:T(128)S(1)}, s32[8]{0:T(128)}, u32[]{:S(2)}) copy-start(s32[8]{0:T(128)} %param.11) | copy-start | bytes 100
  8.5 13.5 %copy-start = (bf16[1024,256]{1,0:T(8,128)(2,1)S(1)}, bf16[1024,256]{1,0:T(8,128)(2,1)}, u32[]{:S(2)}) copy-start(bf16[1024,256]{1,0:T(8,128)(2,1)} %param.10) | copy-start | bytes 1572868
  10.3 18.3 %copy-start.1 = (bf16[8,128,2,128]{1,3,2,0:T(8,128)(2,1)}, bf16[8,128,2,128]{1,3,2,0:T(8,128)(2,1)S(1)}, u32[]{:S(2)}) copy-start(bf16[8,128,2,128]{1,3,2,0:T(8,128)(2,1)S(1)} %copy.48) | copy-start | bytes 1572868
  10.8 20.9 %copy-start.5 = (s32[8,3]{0,1:T(4,128)S(1)}, s32[8,3]{0,1:T(4,128)}, u32[]{:S(2)}) copy-start(s32[8,3]{0,1:T(4,128)} %param.12) | copy-start | bytes 292
  11.9 16.6 %copy-start.3 = (f32[8,2,128,128]{3,2,1,0:T(8,128)}, f32[8,2,128,128]{3,2,1,0:T(8,128)S(1)}, u32[]{:S(2)}) copy-start(f32[8,2,128,128]{3,2,1,0:T(8,128)S(1)} %fusion.38) | copy-start | bytes 3145732
  13.4 24.6 %collective-permute-start.2 = (bf16[384,256]{1,0:T(8,128)(2,1)}, bf16[384,256]{1,0:T(8,128)(2,1)S(1)}, u32[]{:S(2)}, u32[]{:S(2)}) collective-permute-start(bf16[384,256]{1,0:T(8,128)(2,1)} %slice.79), channel_id=1, source_target_pairs={{0,1},{1,2},{2,3},{3,4},{4,5},{5,6},{6,7},{7,8},{8,9},{9,10},{10,1... | collective-permute-start | bytes 589832 | tf_op jit(solution)/shard_map/ppermute | solution.py:26
  18.1 17.6 %collective-permute-start.1 = (s32[3]{0:T(128)}, s32[3]{0:T(128)}, u32[]{:S(2)}, u32[]{:S(2)}) collective-permute-start(s32[3]{0:T(128)} %slice.61), channel_id=1, source_target_pairs={{0,1},{1,2},{2,3},{3,4},{4,5},{5,6},{6,7},{7,8},{8,9},{9,10},{10,1... | collective-permute-start | bytes 44 | tf_op jit(solution)/shard_map/ppermute | solution.py:26
  22.8 20.3 %collective-permute-start = (bf16[384,256]{1,0:T(8,128)(2,1)}, bf16[384,256]{1,0:T(8,128)(2,1)S(1)}, u32[]{:S(2)}, u32[]{:S(2)}) collective-permute-start(bf16[384,256]{1,0:T(8,128)(2,1)} %slice.57), channel_id=1, source_target_pairs={{0,1},{1,2},{2,3},{3,4},{4,5},{5,6},{6,7},{7,8},{8,9},{9,10},{10,1... | collective-permute-start | bytes 589832 | tf_op jit(solution)/shard_map/ppermute | solution.py:26
  63.1 1.0 copy-start.4
  64.2 59.9 %slice-start = ((f32[8,2,128,128]{3,2,1,0:T(8,128)}), f32[7,2,128,128]{3,2,1,0:T(8,128)S(1)}, s32[]{:S(2)}) async-start(f32[8,2,128,128]{3,2,1,0:T(8,128)} %copy-done.3), calls=%async_computation.1 | async-start | bytes 1835008 | tf_op jit(solution)/shard_map/slice | solution.py:47
  68.0 57.6 %copy-start.2 = (bf16[8,128,2,128]{1,3,2,0:T(8,128)(2,1)S(1)}, bf16[8,128,2,128]{1,3,2,0:T(8,128)(2,1)}, u32[]{:S(2)}) copy-start(bf16[8,128,2,128]{1,3,2,0:T(8,128)(2,1)} %copy-done.1) | copy-start | bytes 1572868
  100.9 53.3 %copy-start.6 = (f32[256]{0:T(256)S(1)}, f32[256]{0:T(256)}, u32[]{:S(2)}) copy-start(f32[256]{0:T(256)} %param.13) | copy-start | bytes 3076
Sparse Core Ops, SparseCore 0:
  12.8 88.0 all-gather.1
where the time goes:
time: 167 us; the launch traced here: 166 us
  other arithmetic  40.8 us (24%)
  waiting for transfers between devices  32.9 us (20%)
  local copies, waits for them, and re-layouts  31 us (19%)
  blocking collectives  26.7 us (16%)
  between operations  13.6 us (8%)
  starting transfers between devices  12 us (7%)
  matrix products  8.16 us (5%)
    all_gather x1, waiting for transfers between devices, carried_in(): gathered = lax.all_gather(part, axis)  32.9 us
    psum x1, blocking collectives, shards(): row_squares = lax.psum(local_squares, 'outer')  26.7 us
    add x24, other arithmetic, add_states(): return earlier + later  22.5 us
    another operation x8, local copies, waits for them, and re-layouts, shards(): jnp.stack([extended_values[place:place + groups_here] for place in range(...  13.2 us
    ppermute x3, starting transfers between devices, from_behind(): lax.ppermute(value, axis, [(source, source + steps) for source in range(f...  12 us
    another operation x8, local copies, waits for them, and re-layouts, shards(): jnp.stack([extended_keys[place:place + groups_here] for place in range(PR...  7.08 us
    another operation x1, other arithmetic, shards(): jnp.stack([extended_values[place:place + groups_here] for place in range(...  6.43 us
    sub x1, other arithmetic, shards(): expd = jnp.exp(scores - largest)  3.88 us
  transfers between devices with their start and end apart: 4, of which 1 were waited for; matrix products, arithmetic and copies ran while one was open for 26% of the time, Pallas kernels for 0%

commit v1 on v0

--- a/solution.py
+++ b/solution.py
@@ -7,6 +7,16 @@
 BLK = 128
 PREV = 3
 WIDTH = 4096
+
+
+def process_grid(payload):
+    h_now, high = (payload, 0)
+    width = jax.lax.axis_size("outer")
+    while 1 << high < width:
+        state_next = jax.lax.ppermute(h_now, "outer", [(ix, ix ^ 1 << high) for ix in range(width)])
+        h_now = h_now + state_next
+        high = high + 1
+    return h_now
 
 
 def carried_in(part, axis, combine, identity):
@@ -107,7 +117,7 @@
     )
     linear_part = inter + intra
     local_squares = jnp.sum(linear_part * linear_part, axis=(2, 3))
-    row_squares = lax.psum(local_squares, "outer")
+    row_squares = process_grid(local_squares)
     normed = linear_part * lax.rsqrt(row_squares / WIDTH + 1e-06)[:, :, None, None]
     result = normed * norm_gain.reshape(local_heads, HD)[None, None] + local_part
     return result.reshape(tok_rows, local_heads * HD).astype(jnp.bfloat16)

time: 167 us -> 181 us (1.084)
  blocking collectives: 26.7 us -> 0 us
  waiting for transfers between devices: 32.9 us -> 53.8 us
  starting transfers between devices: 12 us -> 30.4 us
  matrix products: 8.16 us -> 10.6 us
  local copies, waits for them, and re-layouts: 31 us -> 29 us
    psum x1 -> x0, blocking collectives: 26.7 us -> none  [shards(): row_squares = lax.psum(local_squares, 'outer')]
    all_gather x1, waiting for transfers between devices: 32.9 us -> 52.6 us  [carried_in(): gathered = lax.all_gather(part, axis)]
    ppermute x0 -> x4, starting transfers between devices: none -> 18.5 us  [process_grid(): jax.lax.ppermute(h_now, 'outer', [(ix, ix ^ 1 << high) for ix in range(wi...]
    another operation x8, local copies, waits for them, and re-layouts: 13.2 us -> 8.55 us  [shards(): jnp.stack([extended_values[place:place + groups_here] for place in range(...]
    slice x2 -> x1, local copies, waits for them, and re-layouts: 0.01 us -> 2.18 us  [shards(): running[:-1]]
  transfers between devices with their start and end apart: 4 -> 8, of which waited for: 1 -> 2; matrix products, arithmetic and copies ran while one was open for 26% -> 38% of each run, Pallas kernels for 0% -> 0%
where the time goes in v1:
time: 181 us; the launch traced here: 178 us
  waiting for transfers between devices  53.8 us (30%)
  other arithmetic  40 us (22%)
  starting transfers between devices  30.4 us (17%)
  local copies, waits for them, and re-layouts  29 us (16%)
  between operations  13.7 us (8%)
  matrix products  10.6 us (6%)
    all_gather x1, waiting for transfers between devices, carried_in(): gathered = lax.all_gather(part, axis)  52.6 us
    add x24, other arithmetic, add_states(): return earlier + later  22.5 us
    ppermute x4, starting transfers between devices, process_grid(): jax.lax.ppermute(h_now, 'outer', [(ix, ix ^ 1 << high) for ix in range(wi...  18.5 us
    ppermute x3, starting transfers between devices, from_behind(): lax.ppermute(value, axis, [(source, source + steps) for source in range(f...  12 us
    another operation x8, local copies, waits for them, and re-layouts, shards(): jnp.stack([extended_values[place:place + groups_here] for place in range(...  8.55 us
    another operation x8, local copies, waits for them, and re-layouts, shards(): jnp.stack([extended_keys[place:place + groups_here] for place in range(PR...  7.26 us
    another operation x1, other arithmetic, shards(): jnp.stack([extended_values[place:place + groups_here] for place in range(...  6.26 us
    sub x1, other arithmetic, shards(): expd = jnp.exp(scores - largest)  3.86 us
  transfers between devices with their start and end apart: 8, of which 2 were waited for; matrix products, arithmetic and copies ran while one was open for 38% of the time, Pallas kernels for 0%

profile of v1, /device:TPU:7, one launch (start us, length us, event | category | flops | bytes accessed | tf_op | source)
XLA Modules:
  0.0 178.2 jit_solution(935824034905839882)
XLA Ops:
  11.9 1.6 slice.70
  14.2 4.0 %collective-permute-start.6 = (bf16[384,256]{1,0:T(8,128)(2,1)}, bf16[384,256]{1,0:T(8,128)(2,1)S(1)}, u32[]{:S(2)}, u32[]{:S(2)}) collective-permute-start(bf16[384,256]{1,0:T(8,128)(2,1)} %slice.79), channel_id=1, source_target_pairs={{0,1},{1,2},{2,3},{3,4},{4,5},{5,6},{6,7},{7,8},{8,9},{9,10},{10,1... | collective-permute-start | bytes 589832 | tf_op jit(solution)/shard_map/ppermute | solution.py:36
  18.3 4.0 %collective-permute-start.5 = (s32[3]{0:T(128)S(1)}, s32[3]{0:T(128)S(1)}, u32[]{:S(2)}, u32[]{:S(2)}) collective-permute-start(s32[3]{0:T(128)S(1)} %slice.61), channel_id=1, source_target_pairs={{0,1},{1,2},{2,3},{3,4},{4,5},{5,6},{6,7},{7,8},{8,9},{9,10},{10,1... | collective-permute-start | bytes 44 | tf_op jit(solution)/shard_map/ppermute | solution.py:36
  23.0 4.0 %collective-permute-start.4 = (bf16[384,256]{1,0:T(8,128)(2,1)}, bf16[384,256]{1,0:T(8,128)(2,1)}, u32[]{:S(2)}, u32[]{:S(2)}) collective-permute-start(bf16[384,256]{1,0:T(8,128)(2,1)} %slice.57), channel_id=1, source_target_pairs={{0,1},{1,2},{2,3},{3,4},{4,5},{5,6},{6,7},{7,8},{8,9},{9,10},{10,1... | collective-permute-start | bytes 589832 | tf_op jit(solution)/shard_map/ppermute | solution.py:36
  27.0 2.2 %slice.71 = f32[7,2,128,128]{3,2,1,0:T(8,128)} slice(f32[8,2,128,128]{3,2,1,0:T(8,128)} %fusion.38), slice={[0:7], [0:2], [0:128], [0:128]} | slice | bytes 1835008 | tf_op jit(solution)/shard_map/slice | solution.py:57
  31.4 2.0 %copy.56 = bf16[8,1,128,2,128]{4,2,1,3,0:T(8,128)(2,1)} copy(bf16[8,1,128,2,128]{4,3,2,0,1:T(2,128)(2,1)} %stack.58) | data formatting | bytes 1048576 | tf_op jit(solution)/shard_map/stack | solution.py:79
  33.4 2.0 %copy.52 = bf16[8,1,128,2,128]{2,1,4,3,0:T(2,128)(2,1)} copy(bf16[8,1,128,2,128]{4,3,2,0,1:T(2,128)(2,1)S(1)} %stack.48) | data formatting | bytes 1048576 | tf_op jit(solution)/shard_map/stack | solution.py:82
  35.7 1.4 broadcast_and_fusion
  42.6 1.6 pad_maximum_fusion.1
  45.3 3.9 %fusion.33 = (f32[8,2,128]{2,1,0:T(2,128)S(1)}, f32[8,2,128,512]{2,3,1,0:T(8,128)}) fusion(f32[8,2,512,128]{3,2,1,0:T(8,128)S(1)} %fusion.21, pred[8,128,512]{1,2,0:T(8,128)(4,1)S(1)} %copy-done.2), kind=kOutput, calls=%fused_computation.63 | output fusion | flops 6291967 | bytes 8921088 | tf_op jit(solution)/shard_map/sub | solution.py:103
  49.1 52.6 %all-gather.2.cloned.1.call-done = f32[32,2,128,128]{3,2,1,0:T(8,128)} async-done(((f32[1,2,128,128]{3,2,1,0:T(8,128)}), f32[32,2,128,128]{3,2,1,0:T(8,128)}) %all-gather.2.cloned.1.call-update) | async-done | bytes 4194320 | tf_op jit(solution)/shard_map/all_gather | solution.py:24
  101.7 23.1 %while.10 = (s32[]{:T(128)}, f32[2,128,128]{2,1,0:T(8,128)S(1)}, s32[]{:T(128)}, f32[32,2,128,128]{3,2,1,0:T(8,128)}, s32[]{:T(128)}, /*index=5*/s32[]{:T(128)}, s32[]{:T(128)}) while((s32[]{:T(128)}, f32[2,128,128]{2,1,0:T(8,128)S(1)}, s32[]{:T(128)}, f32[32,2,128,128]{3,2,1,0:T(8,128)}, s32[]{:T(128)}, /*index=5*/s32[]{:T(128)}, ...), condition=%wide.region_2.3_spmd, body=%wide.region_1.2_spmd.sunk | while | flops 32773 | bytes 393331 | solution.py:30
  124.9 2.7 %convolution_bitcast_fusion.2 = f32[8,128,2,128]{1,3,2,0:T(8,128)} fusion(f32[7,2,128,128]{3,2,1,0:T(8,128)} %slice.71, f32[2,128,128]{2,1,0:T(8,128)S(1)} %get-tuple-element.28, bf16[8,128,2,128]{3,2,1,0:T(2,128)(2,1)S(1)} %reshape.86), kind=kOutput, calls=%fused_computation.17 | convolution fusion | flops 67633152 | bytes 2621440 | tf_op jit(solution)/shard_map/cthd,chde->cthe/dot_general | solution.py:108
  127.6 2.9 %multiply_reduce_fusion = (f32[8,128]{1,0:T(8,128)S(1)}, f32[8,128,2,128]{1,3,2,0:T(8,128)}) fusion(f32[8,128,2,128]{1,3,2,0:T(8,128)} %convolution_bitcast_fusion.2, bf16[8,128,2,128]{1,3,2,0:T(8,128)(2,1)S(1)} %copy.48, pred[128,128]{0,1:T(8,128)(4,1)S(1)} %iota_compare_fusion, bf16[8,128,2,128]{3,2,1,0:T(2,128)(2,1)S(1)} %reshape.84, ...), kind=kOutput, calls=%fused_computation.21 | convolution fusion | flops 135527424 | bytes 3690496 | tf_op jit(solution)/shard_map/chts,cshe->cthe/dot_general | solution.py:115
  130.4 5.7 %collective-permute-start = (f32[8,128]{1,0:T(8,128)S(1)}, f32[8,128]{1,0:T(8,128)S(1)}, u32[]{:S(2)}, u32[]{:S(2)}) collective-permute-start(f32[8,128]{1,0:T(8,128)S(1)} %get-tuple-element.49), channel_id=1, source_target_pairs={{0,32},{32,0},{64,96},{96,64},{128,160},{160,128},{192,224},{224,1... | collective-permute-start | bytes 12296 | tf_op jit(solution)/shard_map/ppermute | solution.py:16
  137.1 3.1 %collective-permute-start.1 = (f32[8,128]{1,0:T(8,128)S(1)}, f32[8,128]{1,0:T(8,128)S(1)}, u32[]{:S(2)}, u32[]{:S(2)}) collective-permute-start(f32[8,128]{1,0:T(8,128)S(1)} %add.47), channel_id=1, source_target_pairs={{0,64},{32,96},{64,0},{96,32},{128,192},{160,224},{192,128},{224,1... | collective-permute-start | bytes 12296 | tf_op jit(solution)/shard_map/ppermute | solution.py:16
  141.5 4.0 %collective-permute-start.2 = (f32[8,128]{1,0:T(8,128)S(1)}, f32[8,128]{1,0:T(8,128)S(1)}, u32[]{:S(2)}, u32[]{:S(2)}) collective-permute-start(f32[8,128]{1,0:T(8,128)S(1)} %add.48), channel_id=1, source_target_pairs={{0,128},{32,160},{64,192},{96,224},{128,0},{160,32},{192,64},{224,... | collective-permute-start | bytes 12296 | tf_op jit(solution)/shard_map/ppermute | solution.py:16
  145.8 2.0 %copy.49 = bf16[8,1,128,2,128]{2,1,4,3,0:T(2,128)(2,1)} copy(bf16[8,1,128,2,128]{4,3,2,0,1:T(2,128)(2,1)S(1)} %stack.45) | data formatting | bytes 1048576 | tf_op jit(solution)/shard_map/stack | solution.py:82
  147.9 2.0 %copy.50 = bf16[8,1,128,2,128]{2,1,4,3,0:T(2,128)(2,1)} copy(bf16[8,1,128,2,128]{4,3,2,0,1:T(2,128)(2,1)S(1)} %stack.46) | data formatting | bytes 1048576 | tf_op jit(solution)/shard_map/stack | solution.py:82
  150.1 2.0 %copy.51 = bf16[8,1,128,2,128]{2,1,4,3,0:T(2,128)(2,1)} copy(bf16[8,1,128,2,128]{4,3,2,0,1:T(2,128)(2,1)S(1)} %stack.47) | data formatting | bytes 1048576 | tf_op jit(solution)/shard_map/stack | solution.py:82
  152.1 5.6 %collective-permute-start.3 = (f32[8,128]{1,0:T(8,128)S(1)}, f32[8,128]{1,0:T(8,128)S(1)}, u32[]{:S(2)}, u32[]{:S(2)}) collective-permute-start(f32[8,128]{1,0:T(8,128)S(1)} %add.49), channel_id=1, source_target_pairs={{0,256},{32,288},{64,320},{96,352},{128,384},{160,416},{192,448},{... | collective-permute-start | bytes 12296 | tf_op jit(solution)/shard_map/ppermute | solution.py:16
  157.7 6.3 %pad_maximum_fusion = bf16[8,4,128,2,128]{2,1,4,3,0:T(4,128)(2,1)S(1)} fusion(bf16[8,1,128,2,128]{2,1,4,3,0:T(2,128)(2,1)S(1)} %copy-done.1, bf16[8,1,128,2,128]{2,1,4,3,0:T(2,128)(2,1)} %copy.51, bf16[8,1,128,2,128]{2,1,4,3,0:T(2,128)(2,1)} %copy.50, bf16[8,1,128,2,128]{2,1,4,3,0:T(2,128)(2,1)} %copy.49), kind=kLoop, calls=%fused_computation.6 | loop fusion | flops 8388608 | bytes 4194304 | tf_op jit(solution)/shard_map/stack | solution.py:82
  163.9 2.2 %reshape.87 = bf16[8,512,2,128]{1,3,2,0:T(8,128)(2,1)} reshape(bf16[8,4,128,2,128]{2,1,4,3,0:T(4,128)(2,1)S(1)} %pad_maximum_fusion) | data formatting | bytes 4194304 | tf_op jit(solution)/shard_map/reshape | solution.py:84
  166.2 3.8 %fusion.10 = bf16[8,128,2,128]{1,3,2,0:T(8,128)(2,1)S(1)} fusion(bf16[8,512,2,128]{1,3,2,0:T(8,128)(2,1)} %reshape.87, f32[8,2,128,512]{2,3,1,0:T(8,128)} %get-tuple-element.48, f32[8,2,128]{2,1,0:T(2,128)S(1)} %get-tuple-element.47, f32[8,128,2,128]{1,3,2,0:T(8,128)} %get-tuple-element.50, f32[2,128]{1,0:T(2,128)S(1)} %bitcast.65, ...), kind=kOutput, calls=%fused_computation.19 | convolution fusion | flops 271581184 | bytes 7877632 | tf_op jit(solution)/shard_map/chts,cshd->cthd/dot_general | solution.py:105
  (88 shorter events, 42.3 us)
Async XLA Ops:
  6.5 95.2 %all-gather.2.cloned.1.call-start = ((), (), s32[]{:S(2)}) async-start(), calls=%async_computation | async-start | bytes 4325376 | tf_op jit(solution)/shard_map/all_gather | solution.py:24
  8.5 9.7 %copy-start.5 = (s32[8]{0:T(128)S(1)}, s32[8]{0:T(128)}, u32[]{:S(2)}) copy-start(s32[8]{0:T(128)} %param.11) | copy-start | bytes 100
  8.5 13.7 %copy-start = (bf16[1024,256]{1,0:T(8,128)(2,1)S(1)}, bf16[1024,256]{1,0:T(8,128)(2,1)}, u32[]{:S(2)}) copy-start(bf16[1024,256]{1,0:T(8,128)(2,1)} %param.10) | copy-start | bytes 1572868
  10.8 22.5 %copy-start.3 = (s32[8,3]{0,1:T(4,128)S(1)}, s32[8,3]{0,1:T(4,128)}, u32[]{:S(2)}) copy-start(s32[8,3]{0,1:T(4,128)} %param.12) | copy-start | bytes 292
  14.2 22.9 %collective-permute-start.6 = (bf16[384,256]{1,0:T(8,128)(2,1)}, bf16[384,256]{1,0:T(8,128)(2,1)S(1)}, u32[]{:S(2)}, u32[]{:S(2)}) collective-permute-start(bf16[384,256]{1,0:T(8,128)(2,1)} %slice.79), channel_id=1, source_target_pairs={{0,1},{1,2},{2,3},{3,4},{4,5},{5,6},{6,7},{7,8},{8,9},{9,10},{10,1... | collective-permute-start | bytes 589832 | tf_op jit(solution)/shard_map/ppermute | solution.py:36
  18.3 17.2 %collective-permute-start.5 = (s32[3]{0:T(128)S(1)}, s32[3]{0:T(128)S(1)}, u32[]{:S(2)}, u32[]{:S(2)}) collective-permute-start(s32[3]{0:T(128)S(1)} %slice.61), channel_id=1, source_target_pairs={{0,1},{1,2},{2,3},{3,4},{4,5},{5,6},{6,7},{7,8},{8,9},{9,10},{10,1... | collective-permute-start | bytes 44 | tf_op jit(solution)/shard_map/ppermute | solution.py:36
  23.0 113.2 %collective-permute-start.4 = (bf16[384,256]{1,0:T(8,128)(2,1)}, bf16[384,256]{1,0:T(8,128)(2,1)}, u32[]{:S(2)}, u32[]{:S(2)}) collective-permute-start(bf16[384,256]{1,0:T(8,128)(2,1)} %slice.57), channel_id=1, source_target_pairs={{0,1},{1,2},{2,3},{3,4},{4,5},{5,6},{6,7},{7,8},{8,9},{9,10},{10,1... | collective-permute-start | bytes 589832 | tf_op jit(solution)/shard_map/ppermute | solution.py:36
  44.2 1.1 copy-start.2
  130.4 6.7 %collective-permute-start = (f32[8,128]{1,0:T(8,128)S(1)}, f32[8,128]{1,0:T(8,128)S(1)}, u32[]{:S(2)}, u32[]{:S(2)}) collective-permute-start(f32[8,128]{1,0:T(8,128)S(1)} %get-tuple-element.49), channel_id=1, source_target_pairs={{0,32},{32,0},{64,96},{96,64},{128,160},{160,128},{192,224},{224,1... | collective-permute-start | bytes 12296 | tf_op jit(solution)/shard_map/ppermute | solution.py:16
  137.1 4.4 %collective-permute-start.1 = (f32[8,128]{1,0:T(8,128)S(1)}, f32[8,128]{1,0:T(8,128)S(1)}, u32[]{:S(2)}, u32[]{:S(2)}) collective-permute-start(f32[8,128]{1,0:T(8,128)S(1)} %add.47), channel_id=1, source_target_pairs={{0,64},{32,96},{64,0},{96,32},{128,192},{160,224},{192,128},{224,1... | collective-permute-start | bytes 12296 | tf_op jit(solution)/shard_map/ppermute | solution.py:16
  141.5 10.6 %collective-permute-start.2 = (f32[8,128]{1,0:T(8,128)S(1)}, f32[8,128]{1,0:T(8,128)S(1)}, u32[]{:S(2)}, u32[]{:S(2)}) collective-permute-start(f32[8,128]{1,0:T(8,128)S(1)} %add.48), channel_id=1, source_target_pairs={{0,128},{32,160},{64,192},{96,224},{128,0},{160,32},{192,64},{224,... | collective-permute-start | bytes 12296 | tf_op jit(solution)/shard_map/ppermute | solution.py:16
  145.6 12.0 %copy-start.1 = (bf16[8,1,128,2,128]{2,1,4,3,0:T(2,128)(2,1)S(1)}, bf16[8,1,128,2,128]{2,1,4,3,0:T(2,128)(2,1)}, u32[]{:S(2)}) copy-start(bf16[8,1,128,2,128]{2,1,4,3,0:T(2,128)(2,1)} %copy.52) | copy-start | bytes 1572868
  152.1 14.1 %copy-start.4 = (f32[256]{0:T(256)S(1)}, f32[256]{0:T(256)}, u32[]{:S(2)}) copy-start(f32[256]{0:T(256)} %param.13) | copy-start | bytes 3076
  152.1 14.1 %collective-permute-start.3 = (f32[8,128]{1,0:T(8,128)S(1)}, f32[8,128]{1,0:T(8,128)S(1)}, u32[]{:S(2)}, u32[]{:S(2)}) collective-permute-start(f32[8,128]{1,0:T(8,128)S(1)} %add.49), channel_id=1, source_target_pairs={{0,256},{32,288},{64,320},{96,352},{128,384},{160,416},{192,448},{... | collective-permute-start | bytes 12296 | tf_op jit(solution)/shard_map/ppermute | solution.py:16
Sparse Core Ops, SparseCore 0:
  13.6 88.0 all-gather.1
